TPU v7x, 128 devices: a whole 4x4x4 slice. The times are simulated.
128 devices in a mesh: section: 4 (over y), dp: 32 (over x, z, core).
Axes of the slice: x: 4, y: 4, z: 4, core: 2. Of those that a mesh axis runs over, the one named last changes fastest.
Arguments:
- tokens: bfloat16 [8192, 4096], P('dp'), may hold values from -6 to 6
- cotangent: bfloat16 [8192, 4096], P('dp'), may hold values from -30 to 30
- lengths: int32 [128], P('dp'), may hold values from 1 to 64
- seq_user: int32 [128], P('dp'), may hold values from 0 to 63, as said below
- norm_gains: float32 [4, 4096], P('section'), may hold values from 0.5 to 1.5
- weights: float32 [4, 4096, 2, 256], P('section', 'dp'), may hold values from -1 to 1
- first_moment: float32 [4, 4096, 2, 256], P('section', 'dp'), may hold values from -6 to 6
- second_moment: float32 [4, 4096, 2, 256], P('section', 'dp'), may hold values from 0.25 to 4
Outputs:
- new_first: float32 [4, 4096, 2, 256], P('section', 'dp')
- new_second: float32 [4, 4096, 2, 256], P('section', 'dp')
- step_dir: float32 [4, 4096, 2, 256], P('section', 'dp')
- user_ratio: float32 [64], P('dp')
Inputs may be any that keep to these rules, and one draw needn't show every extreme that they name: `seq_user`: the i-th block of 4 sequences carries only the user ids i * 2 to i * 2 + 1, each of them at least once.
All inputs are finite; a program needn't handle non-finite values.
Results may differ from a plain program's by a relative error of at most 0.0045.
Values may be sent and summed in bfloat16 or wider, within the bound.
No kernel may reach another device: no remote copies, remote signals or barrier semaphores. Data moves between devices by JAX's collectives and lax.ppermute only.
A program may use at most 128 MiB of HBM per device.

v0:
```python
import jax
import jax.numpy as jnp
from jax import lax
from jax.sharding import PartitionSpec as P

SEQLEN = 64
USERS_DEV = 2
CLIP_BOUND = 70000.0
LOSS_SCALE = 1024.0
BETA_ONE = 0.9
BETA_TWO = 0.999
FIRST_FIX = 1.0 - 0.9**50
SECOND_FIX = 1.0 - 0.999**50
ADAM_EPS = 1e-08
NORM_EPS = 1e-05


def passed_along(value, axis, steps):
    count = lax.axis_size(axis)
    initial, last = (max(0, -steps), min(count, count - steps))
    return lax.ppermute(value, axis, [(source, source + steps) for source in range(initial, last)])


def section_forward(hidden, section_gain, down_cast, up_cast):
    widened = hidden.astype(jnp.float32)
    inverse = lax.rsqrt(jnp.mean(widened * widened, axis=-1, keepdims=True) + NORM_EPS)
    normed = (widened * inverse * section_gain).astype(jnp.bfloat16)
    inner_act = jnp.dot(normed, down_cast, preferred_element_type=jnp.float32)
    active = jax.nn.silu(inner_act).astype(jnp.bfloat16)
    branch = lax.dot_general(
        active, up_cast, (((1,), (1,)), ((), ())), preferred_element_type=jnp.float32
    )
    return ((widened + branch).astype(jnp.bfloat16), (widened, inverse, normed, inner_act, active))


def section_backward(grad_out, section_gain, down_cast, up_cast, kept_acts):
    widened, inverse, normed, inner_act, active = kept_acts
    grad_active = jnp.dot(grad_out, up_cast, preferred_element_type=jnp.float32)
    sigmoid_val = jax.nn.sigmoid(inner_act)
    grad_inner = (grad_active * sigmoid_val * (1.0 + inner_act * (1.0 - sigmoid_val))).astype(
        jnp.bfloat16
    )
    grad_normed = lax.dot_general(
        grad_inner, down_cast, (((1,), (1,)), ((), ())), preferred_element_type=jnp.float32
    )
    scaled = grad_normed * section_gain
    projected = jnp.mean(scaled * widened, axis=-1, keepdims=True)
    grad_in = (
        grad_out.astype(jnp.float32)
        + inverse * scaled
        - widened * inverse * inverse * inverse * projected
    )
    return (grad_in.astype(jnp.bfloat16), grad_inner)


def gram_of(values):
    return lax.dot_general(
        values, values, (((1,), (1,)), ((), ())), preferred_element_type=jnp.float32
    )


def user_squares(normed, grad_inner, active, grad_out, owners):
    joint = gram_of(normed) * gram_of(grad_inner) + gram_of(active) * gram_of(grad_out)
    spread = jnp.dot(joint, owners, precision=lax.Precision.HIGHEST)
    return jnp.sum(spread * owners, axis=0)


def keep_block(stored, produced, block_slot, blocks):
    usable = (block_slot >= 0) & (block_slot < blocks)
    clamped = jnp.clip(block_slot, 0, blocks - 1)
    if stored is None:
        stored = tuple(
            (jnp.zeros((blocks,) + element.shape, element.dtype) for element in produced)
        )
    updated = []
    for buffer, element in zip(stored, produced):
        before = lax.dynamic_index_in_dim(buffer, clamped, 0, keepdims=False)
        updated.append(
            lax.dynamic_update_index_in_dim(buffer, jnp.where(usable, element, before), clamped, 0)
        )
    return tuple(updated)


def active_width(stored):
    return stored[4].shape[-1]


def on_device(
    tokens, cotangent, lengths, seq_user, norm_gains, weights, first_moment, second_moment
):
    section_count = lax.axis_size("section")
    section_index = lax.axis_index("section")
    blocks = 1
    tok_rows = tokens.shape[0]
    model_width = tokens.shape[1]
    block_rows = tok_rows // blocks
    rounds = blocks + section_count - 1
    section_gain = norm_gains[0]
    packed = lax.all_gather(weights.astype(jnp.bfloat16), "dp", axis=1, tiled=True)
    down_cast = packed[0, :, 0, :]
    up_cast = packed[0, :, 1, :]
    inputs = tokens.reshape(blocks, block_rows, model_width)
    carried = jnp.zeros((block_rows, model_width), jnp.bfloat16)
    stored = None
    for step_no in range(rounds):
        incoming = jnp.where(section_index == 0, inputs[min(step_no, blocks - 1)], carried)
        result, kept_acts = section_forward(incoming, section_gain, down_cast, up_cast)
        stored = keep_block(stored, kept_acts, step_no - section_index, blocks)
        if step_no + 1 < rounds:
            carried = passed_along(result, "section", 1)
    positions = jnp.arange(tok_rows) % SEQLEN
    usable = positions < jnp.repeat(lengths, SEQLEN)
    local_user = seq_user - lax.axis_index("dp") * USERS_DEV
    token_user = jnp.repeat(local_user, SEQLEN)
    owners = ((token_user[:, None] == jnp.arange(USERS_DEV)[None, :]) & usable[:, None]).astype(
        jnp.float32
    )
    seed_rows = (cotangent * usable[:, None].astype(jnp.bfloat16)).reshape(
        blocks, block_rows, model_width
    )
    carried = jnp.zeros((block_rows, model_width), jnp.bfloat16)
    grad_store = None
    for step_no in range(rounds):
        block_slot = step_no - (section_count - 1 - section_index)
        clamped = jnp.clip(block_slot, 0, blocks - 1)
        incoming = jnp.where(
            section_index == section_count - 1, seed_rows[min(step_no, blocks - 1)], carried
        )
        kept_acts = tuple(
            (lax.dynamic_index_in_dim(buffer, clamped, 0, keepdims=False) for buffer in stored)
        )
        grad_in, grad_inner = section_backward(
            incoming, section_gain, down_cast, up_cast, kept_acts
        )
        grad_store = keep_block(grad_store, (incoming, grad_inner), block_slot, blocks)
        if step_no + 1 < rounds:
            carried = passed_along(grad_in, "section", -1)
    normed_all = stored[2].reshape(tok_rows, model_width)
    active_all = stored[4].reshape(tok_rows, active_width(stored))
    grad_out_all = grad_store[0].reshape(tok_rows, model_width)
    grad_inner_all = grad_store[1].reshape(tok_rows, active_width(stored))
    local_squares = user_squares(normed_all, grad_inner_all, active_all, grad_out_all, owners)
    squares = lax.psum(local_squares, "section")
    user_norm = jnp.sqrt(squares)
    factors = LOSS_SCALE / jnp.maximum(user_norm, CLIP_BOUND)
    token_factor = jnp.dot(owners, factors, precision=lax.Precision.HIGHEST)
    weighted_inner = (grad_inner_all.astype(jnp.float32) * token_factor[:, None]).astype(
        jnp.bfloat16
    )
    weighted_out = (grad_out_all.astype(jnp.float32) * token_factor[:, None]).astype(jnp.bfloat16)
    down_term = lax.dot_general(
        normed_all, weighted_inner, (((0,), (0,)), ((), ())), preferred_element_type=jnp.float32
    )
    up_term = lax.dot_general(
        weighted_out, active_all, (((0,), (0,)), ((), ())), preferred_element_type=jnp.float32
    )
    gradient = lax.psum_scatter(
        jnp.stack([down_term, up_term], axis=1).astype(jnp.bfloat16),
        "dp",
        scatter_dimension=0,
        tiled=True,
    ).astype(jnp.float32)
    moment_one = BETA_ONE * first_moment[0] + (1.0 - BETA_ONE) * gradient
    moment_two = BETA_TWO * second_moment[0] + (1.0 - BETA_TWO) * gradient * gradient
    direction = moment_one / FIRST_FIX / (jnp.sqrt(moment_two / SECOND_FIX) + ADAM_EPS)
    return (moment_one[None], moment_two[None], direction[None], user_norm / CLIP_BOUND)


def solution(mesh):
    return jax.shard_map(
        on_device,
        mesh=mesh,
        in_specs=(
            P("dp", None),
            P("dp", None),
            P("dp"),
            P("dp"),
            P("section", None),
            P("section", "dp", None, None),
            P("section", "dp", None, None),
            P("section", "dp", None, None),
        ),
        out_specs=(
            P("section", "dp", None, None),
            P("section", "dp", None, None),
            P("section", "dp", None, None),
            P("dp"),
        ),
        check_vma=False,
    )
```

profile of v0, /device:TPU:0, one launch (start us, length us, event | category | flops | bytes accessed | tf_op | source)
XLA Modules:
  0.0 489.0 jit_solution(7578786689394321223)
XLA Ops:
  9.1 2.2 fusion.8
  11.3 48.3 %all-gather.2.cloned.1.call-done = bf16[1,4096,2,256]{3,1,2,0:T(8,128)(2,1)} async-done(((bf16[1,128,2,256]{3,1,2,0:T(8,128)(2,1)}), bf16[1,4096,2,256]{3,1,2,0:T(8,128)(2,1)}) %all-gather.2.cloned.1.call-update) | async-done | bytes 4194320 | tf_op jit(solution)/shard_map/all_gather | solution.py:99
  59.6 2.5 fusion.35
  63.2 3.5 collective-permute-start
  66.8 45.1 %collective-permute-done = bf16[256,4096]{1,0:T(8,128)(2,1)S(1)} collective-permute-done((bf16[256,4096]{1,0:T(8,128)(2,1)S(1)}, bf16[256,4096]{1,0:T(8,128)(2,1)S(1)}, u32[]{:S(2)}, u32[]{:S(2)}) %collective-permute-start) | collective-permute-done | bytes 2097184 | tf_op jit(solution)/shard_map/ppermute | solution.py:21
  114.9 4.5 collective-permute-start.1
  119.5 44.3 %collective-permute-done.1 = bf16[256,4096]{1,0:T(8,128)(2,1)S(1)} collective-permute-done((bf16[256,4096]{1,0:T(8,128)(2,1)S(1)}, bf16[256,4096]{1,0:T(8,128)(2,1)S(1)}, u32[]{:S(2)}, u32[]{:S(2)}) %collective-permute-start.1) | collective-permute-done | bytes 2097184 | tf_op jit(solution)/shard_map/ppermute | solution.py:21
  166.1 2.1 fusion.2
  168.2 5.7 %collective-permute-start.2 = (bf16[256,4096]{1,0:T(8,128)(2,1)}, bf16[256,4096]{1,0:T(8,128)(2,1)}, u32[]{:S(2)}, u32[]{:S(2)}) collective-permute-start(bf16[256,4096]{1,0:T(8,128)(2,1)} %fusion.2), channel_id=1, source_target_pairs={{0,32},{32,64},{64,96},{1,33},{33,65},{65,97},{2,34},{34,66},{66,9... | collective-permute-start | bytes 6291464 | tf_op jit(solution)/shard_map/ppermute | solution.py:21
  174.1 42.4 %collective-permute-done.2 = bf16[256,4096]{1,0:T(8,128)(2,1)} collective-permute-done((bf16[256,4096]{1,0:T(8,128)(2,1)}, bf16[256,4096]{1,0:T(8,128)(2,1)}, u32[]{:S(2)}, u32[]{:S(2)}) %collective-permute-start.2) | collective-permute-done | bytes 2097184 | tf_op jit(solution)/shard_map/ppermute | solution.py:21
  222.0 2.2 multiply_reduce_fusion.2
  224.2 1.8 subtract_convert_fusion.2
  227.3 48.1 %collective-permute-done.3 = bf16[256,4096]{1,0:T(8,128)(2,1)S(1)} collective-permute-done((bf16[256,4096]{1,0:T(8,128)(2,1)S(1)}, bf16[256,4096]{1,0:T(8,128)(2,1)S(1)}, u32[]{:S(2)}, u32[]{:S(2)}) %collective-permute-start.3) | collective-permute-done | bytes 2097184 | tf_op jit(solution)/shard_map/ppermute | solution.py:21
  277.1 2.3 subtract_convert_fusion.1
  280.7 45.2 %collective-permute-done.4 = bf16[256,4096]{1,0:T(8,128)(2,1)S(1)} collective-permute-done((bf16[256,4096]{1,0:T(8,128)(2,1)S(1)}, bf16[256,4096]{1,0:T(8,128)(2,1)S(1)}, u32[]{:S(2)}, u32[]{:S(2)}) %collective-permute-start.4) | collective-permute-done | bytes 2097184 | tf_op jit(solution)/shard_map/ppermute | solution.py:21
  327.6 3.3 subtract_convert_fusion
  332.8 4.7 select_select_fusion.1
  337.6 39.2 %collective-permute-done.5 = bf16[256,4096]{1,0:T(8,128)(2,1)} collective-permute-done((bf16[256,4096]{1,0:T(8,128)(2,1)}, bf16[256,4096]{1,0:T(8,128)(2,1)}, u32[]{:S(2)}, u32[]{:S(2)}) %collective-permute-start.5) | collective-permute-done | bytes 2097184 | tf_op jit(solution)/shard_map/ppermute | solution.py:21
  376.8 2.4 fusion.29
  379.5 2.3 select_select_fusion
  383.7 8.9 %psum.7 = f32[2]{0:T(128)S(1)} all-reduce(f32[2]{0:T(128)S(1)} %fusion.30), channel_id=1, replica_groups=mesh['section'=4,'dp'=32] {'section'}, use_global_device_ids=true, to_apply=%region_8.9 | all-reduce | flops 2 | bytes 16 | tf_op jit(solution)/shard_map/psum | solution.py:143
  392.8 2.4 fusion.3
  396.2 2.3 pad_maximum_fusion
  399.1 79.3 %reduce-scatter.2.cloned.1.call-done = bf16[128,2,256]{2,0,1:T(8,128)(2,1)} async-done(((bf16[4096,2,256]{2,0,1:T(8,128)(2,1)}), bf16[128,2,256]{2,0,1:T(8,128)(2,1)}) %reduce-scatter.2.cloned.1.call-update) | async-done | bytes 131088 | tf_op jit(solution)/shard_map/reduce_scatter | solution.py:157
  (89 shorter events, 29.2 us)
Async XLA Ops:
  7.2 52.5 %copy-start = (bf16[256,4096]{1,0:T(8,128)(2,1)S(1)}, bf16[256,4096]{1,0:T(8,128)(2,1)}, u32[]{:S(2)}) copy-start(bf16[256,4096]{1,0:T(8,128)(2,1)} %param.8) | copy-start | bytes 6291460
  7.2 52.5 %copy-start.18 = (f32[1,4096]{1,0:T(1,128)S(1)}, f32[1,4096]{1,0:T(1,128)}, u32[]{:S(2)}) copy-start(f32[1,4096]{1,0:T(1,128)} %param.12) | copy-start | bytes 49156
  7.2 52.5 %all-gather.2.cloned.1.call-start = ((), (), s32[]{:S(2)}) async-start(), calls=%async_computation.1 | async-start | bytes 4325376 | tf_op jit(solution)/shard_map/all_gather | solution.py:99
  9.0 469.4 %reduce-scatter.2.cloned.1.call-start = ((), (), s32[]{:S(2)}) async-start(), calls=%async_computation.2 | async-start | bytes 4325376 | tf_op jit(solution)/shard_map/reduce_scatter | solution.py:157
  59.6 2.8 copy-start.13
  63.2 48.7 %collective-permute-start = (bf16[256,4096]{1,0:T(8,128)(2,1)S(1)}, bf16[256,4096]{1,0:T(8,128)(2,1)S(1)}, u32[]{:S(2)}, u32[]{:S(2)}) collective-permute-start(bf16[256,4096]{1,0:T(8,128)(2,1)S(1)} %fusion), channel_id=1, source_target_pairs={{0,32},{32,64},{64,96},{1,33},{33,65},{65,97},{2,34},{34,66},{66,9... | collective-permute-start | bytes 6291464 | tf_op jit(solution)/shard_map/ppermute | solution.py:21
  114.9 48.8 %collective-permute-start.1 = (bf16[256,4096]{1,0:T(8,128)(2,1)S(1)}, bf16[256,4096]{1,0:T(8,128)(2,1)S(1)}, u32[]{:S(2)}, u32[]{:S(2)}) collective-permute-start(bf16[256,4096]{1,0:T(8,128)(2,1)S(1)} %fusion.1), channel_id=1, source_target_pairs={{0,32},{32,64},{64,96},{1,33},{33,65},{65,97},{2,34},{34,66},{66,9... | collective-permute-start | bytes 6291464 | tf_op jit(solution)/shard_map/ppermute | solution.py:21
  166.1 7.8 %copy-start.19 = (s32[4]{0:T(128)S(1)}, s32[4]{0:T(128)}, u32[]{:S(2)}) copy-start(s32[4]{0:T(128)} %param.10) | copy-start | bytes 52
  168.2 48.3 %collective-permute-start.2 = (bf16[256,4096]{1,0:T(8,128)(2,1)}, bf16[256,4096]{1,0:T(8,128)(2,1)}, u32[]{:S(2)}, u32[]{:S(2)}) collective-permute-start(bf16[256,4096]{1,0:T(8,128)(2,1)} %fusion.2), channel_id=1, source_target_pairs={{0,32},{32,64},{64,96},{1,33},{33,65},{65,97},{2,34},{34,66},{66,9... | collective-permute-start | bytes 6291464 | tf_op jit(solution)/shard_map/ppermute | solution.py:21
  174.1 43.4 %copy-start.14 = (bf16[1,4096,2,256]{3,1,2,0:T(8,128)(2,1)S(1)}, bf16[1,4096,2,256]{3,1,2,0:T(8,128)(2,1)}, u32[]{:S(2)}) copy-start(bf16[1,4096,2,256]{3,1,2,0:T(8,128)(2,1)} %all-gather.2.cloned.1.call-done) | copy-start | bytes 12582916
  217.4 3.1 copy-start.8
  217.4 2.3 copy-start.1
  219.8 2.2 copy-start.7
  226.0 49.4 %collective-permute-start.3 = (bf16[256,4096]{1,0:T(8,128)(2,1)S(1)}, bf16[256,4096]{1,0:T(8,128)(2,1)S(1)}, u32[]{:S(2)}, u32[]{:S(2)}) collective-permute-start(bf16[256,4096]{1,0:T(8,128)(2,1)S(1)} %subtract_convert_fusion.2), channel_id=1, source_target_pairs={{32,0},{64,32},{96,64},{33,1},{65,33},{97,65},{34,2},{66,34},{98,6... | collective-permute-start | bytes 6291464 | tf_op jit(solution)/shard_map/ppermute | solution.py:21
  279.4 46.5 %collective-permute-start.4 = (bf16[256,4096]{1,0:T(8,128)(2,1)S(1)}, bf16[256,4096]{1,0:T(8,128)(2,1)S(1)}, u32[]{:S(2)}, u32[]{:S(2)}) collective-permute-start(bf16[256,4096]{1,0:T(8,128)(2,1)S(1)} %subtract_convert_fusion.1), channel_id=1, source_target_pairs={{32,0},{64,32},{96,64},{33,1},{65,33},{97,65},{34,2},{66,34},{98,6... | collective-permute-start | bytes 6291464 | tf_op jit(solution)/shard_map/ppermute | solution.py:21
  327.5 4.8 copy-start.20
  330.8 46.0 %collective-permute-start.5 = (bf16[256,4096]{1,0:T(8,128)(2,1)}, bf16[256,4096]{1,0:T(8,128)(2,1)}, u32[]{:S(2)}, u32[]{:S(2)}) collective-permute-start(bf16[256,4096]{1,0:T(8,128)(2,1)} %subtract_convert_fusion), channel_id=1, source_target_pairs={{32,0},{64,32},{96,64},{33,1},{65,33},{97,65},{34,2},{66,34},{98,6... | collective-permute-start | bytes 6291464 | tf_op jit(solution)/shard_map/ppermute | solution.py:21
  332.8 44.0 %copy-start.2 = (bf16[256,4096]{1,0:T(8,128)(2,1)S(1)}, bf16[256,4096]{1,0:T(8,128)(2,1)}, u32[]{:S(2)}) copy-start(bf16[256,4096]{1,0:T(8,128)(2,1)} %param.9) | copy-start | bytes 6291460
  332.8 44.0 %copy-start.15 = (bf16[1,4096,2,256]{3,1,2,0:T(8,128)(2,1)S(1)}, bf16[1,4096,2,256]{3,1,2,0:T(8,128)(2,1)}, u32[]{:S(2)}) copy-start(bf16[1,4096,2,256]{3,1,2,0:T(8,128)(2,1)} %all-gather.2.cloned.1.call-done) | copy-start | bytes 12582916
  337.6 45.0 %copy-start.3 = (bf16[256,4096]{1,0:T(8,128)(2,1)}, bf16[256,4096]{1,0:T(8,128)(2,1)S(1)}, u32[]{:S(2)}) copy-start(bf16[256,4096]{1,0:T(8,128)(2,1)S(1)} %select_select_fusion.1) | copy-start | bytes 6291460
  337.6 41.9 %copy-start.10 = (bf16[256,4096]{1,0:T(8,128)(2,1)S(1)}, bf16[256,4096]{1,0:T(8,128)(2,1)}, u32[]{:S(2)}) copy-start(bf16[256,4096]{1,0:T(8,128)(2,1)} %copy-done.9) | copy-start | bytes 6291460
  337.6 41.9 %copy-start.12 = (bf16[256,4096]{1,0:T(8,128)(2,1)S(1)}, bf16[256,4096]{1,0:T(8,128)(2,1)}, u32[]{:S(2)}) copy-start(bf16[256,4096]{1,0:T(8,128)(2,1)} %copy-done.11) | copy-start | bytes 6291460
  398.5 79.8 %copy-start.16 = (f32[1,128,2,256]{3,2,1,0:T(2,128)S(1)}, f32[1,128,2,256]{3,2,1,0:T(2,128)}, u32[]{:S(2)}) copy-start(f32[1,128,2,256]{3,2,1,0:T(2,128)} %param.14) | copy-start | bytes 786436
  398.5 79.8 %copy-start.17 = (f32[1,128,2,256]{3,2,1,0:T(2,128)S(1)}, f32[1,128,2,256]{3,2,1,0:T(2,128)}, u32[]{:S(2)}) copy-start(f32[1,128,2,256]{3,2,1,0:T(2,128)} %param.15) | copy-start | bytes 786436
  (5 other events, 7.6 us)
Sparse Core Ops, SparseCore 0:
  10.9 48.6 all-gather.1
  398.7 79.6 reduce-scatter.1
where the time goes:
time: 490 us; the launch traced here: 489 us
  waiting for transfers between devices  392 us (80%)
  other arithmetic  23.6 us (5%)
  matrix products  23.1 us (5%)
  starting transfers between devices  17.9 us (4%)
  between operations  14.5 us (3%)
  local copies, waits for them, and re-layouts  8.95 us (2%)
  blocking collectives  8.92 us (2%)
    ppermute x6, waiting for transfers between devices, passed_along(): lax.ppermute(value, axis, [(source, source + steps) for source in range(i...  264 us
    reduce_scatter x1, waiting for transfers between devices, on_device(): lax.psum_scatter(jnp.stack([down_term, up_term], axis=1).astype(jnp.bfloa...  79.3 us
    all_gather x1, waiting for transfers between devices, on_device(): lax.all_gather(weights.astype(jnp.bfloat16), 'dp', axis=1, tiled=True)  48.3 us
    ppermute x6, starting transfers between devices, passed_along(): lax.ppermute(value, axis, [(source, source + steps) for source in range(i...  17.8 us
  transfers between devices with their start and end apart: 8, of which 8 were waited for; matrix products, arithmetic and copies ran while one was open for 2% of the time, Pallas kernels for 0%

commit v1 on v0

--- a/solution.py
+++ b/solution.py
@@ -96,7 +96,10 @@
     block_rows = tok_rows // blocks
     rounds = blocks + section_count - 1
     section_gain = norm_gains[0]
-    packed = lax.all_gather(weights.astype(jnp.bfloat16), "dp", axis=1, tiled=True)
+    packed = jnp.concatenate(
+        lax.all_to_all(jnp.stack([weights.astype(jnp.bfloat16)] * lax.axis_size("dp")), "dp", 0, 0),
+        axis=1,
+    )
     down_cast = packed[0, :, 0, :]
     up_cast = packed[0, :, 1, :]
     inputs = tokens.reshape(blocks, block_rows, model_width)

time: 490 us -> 504 us (1.029)
  starting transfers between devices: 17.9 us -> 26.5 us
    all_to_all x0 -> x1, waiting for transfers between devices: none -> 51.7 us  [on_device(): lax.all_to_all(jnp.stack([weights.astype(jnp.bfloat16)] * lax.axis_size('...]
    all_gather x1 -> x0, waiting for transfers between devices: 48.3 us -> none  [on_device(): lax.all_gather(weights.astype(jnp.bfloat16), 'dp', axis=1, tiled=True)]
    all_to_all x0 -> x1, starting transfers between devices: none -> 8.54 us  [on_device(): lax.all_to_all(jnp.stack([weights.astype(jnp.bfloat16)] * lax.axis_size('...]
  transfers between devices with their start and end apart: 8 -> 8, of which waited for: 8 -> 8; matrix products, arithmetic and copies ran while one was open for 2% -> 1% of each run, Pallas kernels for 0% -> 0%
where the time goes in v1:
time: 504 us
  waiting for transfers between devices  397 us (79%)
  starting transfers between devices  26.5 us (5%)
  other arithmetic  23.1 us (5%)
  matrix products  21.7 us (4%)
  between operations  14.5 us (3%)
  local copies, waits for them, and re-layouts  11.7 us (2%)
  blocking collectives  8.92 us (2%)
    ppermute x6, waiting for transfers between devices, passed_along(): lax.ppermute(value, axis, [(source, source + steps) for source in range(i...  262 us
    reduce_scatter x1, waiting for transfers between devices, on_device(): lax.psum_scatter(jnp.stack([down_term, up_term], axis=1).astype(jnp.bfloa...  83.4 us
    all_to_all x1, waiting for transfers between devices, on_device(): lax.all_to_all(jnp.stack([weights.astype(jnp.bfloat16)] * lax.axis_size('...  51.7 us
    ppermute x6, starting transfers between devices, passed_along(): lax.ppermute(value, axis, [(source, source + steps) for source in range(i...  17.9 us
  transfers between devices with their start and end apart: 8, of which 8 were waited for; matrix products, arithmetic and copies ran while one was open for 1% of the time, Pallas kernels for 0%

profile of v1, /device:TPU:0, one launch (start us, length us, event | category | flops | bytes accessed | tf_op | source)
XLA Modules:
  0.0 503.7 jit_solution(13215233353865818902)
XLA Ops:
  8.2 2.5 stack.11
  10.7 8.5 %all-to-all-start = ((bf16[32,1,128,2,256]{4,2,3,1,0:T(8,128)(2,1)}), bf16[32,1,128,2,256]{4,2,3,1,0:T(8,128)(2,1)}, u32[]{:S(2)}, u32[]{:S(2)}) async-start(bf16[32,1,128,2,256]{4,2,3,1,0:T(8,128)(2,1)} %stack.11), calls=%async_computation | async-start | bytes 8388608 | tf_op jit(solution)/shard_map/all_to_all | solution.py:100
  20.0 51.7 %all-to-all-done = bf16[32,1,128,2,256]{4,2,3,1,0:T(8,128)(2,1)} async-done(((bf16[32,1,128,2,256]{4,2,3,1,0:T(8,128)(2,1)}), bf16[32,1,128,2,256]{4,2,3,1,0:T(8,128)(2,1)}, u32[]{:S(2)}, u32[]{:S(2)}) %all-to-all-start) | async-done | bytes 4194336 | tf_op jit(solution)/shard_map/all_to_all | solution.py:100
  71.7 2.5 copy.25
  75.8 3.6 collective-permute-start
  79.5 44.8 %collective-permute-done = bf16[256,4096]{1,0:T(8,128)(2,1)S(1)} collective-permute-done((bf16[256,4096]{1,0:T(8,128)(2,1)S(1)}, bf16[256,4096]{1,0:T(8,128)(2,1)S(1)}, u32[]{:S(2)}, u32[]{:S(2)}) %collective-permute-start) | collective-permute-done | bytes 2097184 | tf_op jit(solution)/shard_map/ppermute | solution.py:21
  127.3 4.5 collective-permute-start.1
  131.8 43.9 %collective-permute-done.1 = bf16[256,4096]{1,0:T(8,128)(2,1)S(1)} collective-permute-done((bf16[256,4096]{1,0:T(8,128)(2,1)S(1)}, bf16[256,4096]{1,0:T(8,128)(2,1)S(1)}, u32[]{:S(2)}, u32[]{:S(2)}) %collective-permute-start.1) | collective-permute-done | bytes 2097184 | tf_op jit(solution)/shard_map/ppermute | solution.py:21
  178.1 2.2 fusion.2
  180.2 5.7 %collective-permute-start.2 = (bf16[256,4096]{1,0:T(8,128)(2,1)}, bf16[256,4096]{1,0:T(8,128)(2,1)}, u32[]{:S(2)}, u32[]{:S(2)}) collective-permute-start(bf16[256,4096]{1,0:T(8,128)(2,1)} %fusion.2), channel_id=1, source_target_pairs={{0,32},{32,64},{64,96},{1,33},{33,65},{65,97},{2,34},{34,66},{66,9... | collective-permute-start | bytes 6291464 | tf_op jit(solution)/shard_map/ppermute | solution.py:21
  186.1 42.0 %collective-permute-done.2 = bf16[256,4096]{1,0:T(8,128)(2,1)} collective-permute-done((bf16[256,4096]{1,0:T(8,128)(2,1)}, bf16[256,4096]{1,0:T(8,128)(2,1)}, u32[]{:S(2)}, u32[]{:S(2)}) %collective-permute-start.2) | collective-permute-done | bytes 2097184 | tf_op jit(solution)/shard_map/ppermute | solution.py:21
  233.6 2.2 multiply_reduce_fusion.2
  239.0 47.8 %collective-permute-done.3 = bf16[256,4096]{1,0:T(8,128)(2,1)S(1)} collective-permute-done((bf16[256,4096]{1,0:T(8,128)(2,1)S(1)}, bf16[256,4096]{1,0:T(8,128)(2,1)S(1)}, u32[]{:S(2)}, u32[]{:S(2)}) %collective-permute-start.3) | collective-permute-done | bytes 2097184 | tf_op jit(solution)/shard_map/ppermute | solution.py:21
  288.4 2.3 subtract_convert_fusion.1
  292.0 44.8 %collective-permute-done.4 = bf16[256,4096]{1,0:T(8,128)(2,1)S(1)} collective-permute-done((bf16[256,4096]{1,0:T(8,128)(2,1)S(1)}, bf16[256,4096]{1,0:T(8,128)(2,1)S(1)}, u32[]{:S(2)}, u32[]{:S(2)}) %collective-permute-start.4) | collective-permute-done | bytes 2097184 | tf_op jit(solution)/shard_map/ppermute | solution.py:21
  338.5 3.3 subtract_convert_fusion
  343.7 4.7 select_select_fusion.1
  348.5 38.9 %collective-permute-done.5 = bf16[256,4096]{1,0:T(8,128)(2,1)} collective-permute-done((bf16[256,4096]{1,0:T(8,128)(2,1)}, bf16[256,4096]{1,0:T(8,128)(2,1)}, u32[]{:S(2)}, u32[]{:S(2)}) %collective-permute-start.5) | collective-permute-done | bytes 2097184 | tf_op jit(solution)/shard_map/ppermute | solution.py:21
  387.4 2.4 fusion.29
  390.1 2.3 select_select_fusion
  394.3 8.9 %psum.7 = f32[2]{0:T(128)S(1)} all-reduce(f32[2]{0:T(128)S(1)} %fusion.30), channel_id=1, replica_groups=mesh['section'=4,'dp'=32] {'section'}, use_global_device_ids=true, to_apply=%region_8.9 | all-reduce | flops 2 | bytes 16 | tf_op jit(solution)/shard_map/psum | solution.py:146
  403.3 2.4 fusion.3
  406.8 2.3 pad_maximum_fusion
  409.6 83.4 %reduce-scatter.2.cloned.1.call-done = bf16[128,2,256]{2,0,1:T(8,128)(2,1)} async-done(((bf16[4096,2,256]{2,0,1:T(8,128)(2,1)}), bf16[128,2,256]{2,0,1:T(8,128)(2,1)}) %reduce-scatter.2.cloned.1.call-update) | async-done | bytes 131088 | tf_op jit(solution)/shard_map/reduce_scatter | solution.py:160
  (91 shorter events, 31.5 us)
Async XLA Ops:
  10.7 8.6 %copy-start = (bf16[256,4096]{1,0:T(8,128)(2,1)S(1)}, bf16[256,4096]{1,0:T(8,128)(2,1)}, u32[]{:S(2)}) copy-start(bf16[256,4096]{1,0:T(8,128)(2,1)} %param.8) | copy-start | bytes 6291460
  10.7 61.0 %all-to-all-start = ((bf16[32,1,128,2,256]{4,2,3,1,0:T(8,128)(2,1)}), bf16[32,1,128,2,256]{4,2,3,1,0:T(8,128)(2,1)}, u32[]{:S(2)}, u32[]{:S(2)}) async-start(bf16[32,1,128,2,256]{4,2,3,1,0:T(8,128)(2,1)} %stack.11), calls=%async_computation | async-start | bytes 8388608 | tf_op jit(solution)/shard_map/all_to_all | solution.py:100
  19.2 473.8 %reduce-scatter.2.cloned.1.call-start = ((), (), s32[]{:S(2)}) async-start(), calls=%async_computation.2 | async-start | bytes 4325376 | tf_op jit(solution)/shard_map/reduce_scatter | solution.py:160
  20.0 54.2 %copy-start.18 = (f32[1,4096]{1,0:T(1,128)S(1)}, f32[1,4096]{1,0:T(1,128)}, u32[]{:S(2)}) copy-start(f32[1,4096]{1,0:T(1,128)} %param.12) | copy-start | bytes 49156
  74.2 103.4 %copy-start.4 = (bf16[32,1,128,2,256]{4,2,0,3,1:T(8,128)(2,1)}, bf16[32,1,128,2,256]{4,2,0,3,1:T(8,128)(2,1)S(1)}, u32[]{:S(2)}) copy-start(bf16[32,1,128,2,256]{4,2,0,3,1:T(8,128)(2,1)S(1)} %copy.25) | copy-start | bytes 12582916
  75.8 48.4 %collective-permute-start = (bf16[256,4096]{1,0:T(8,128)(2,1)S(1)}, bf16[256,4096]{1,0:T(8,128)(2,1)S(1)}, u32[]{:S(2)}, u32[]{:S(2)}) collective-permute-start(bf16[256,4096]{1,0:T(8,128)(2,1)S(1)} %fusion), channel_id=1, source_target_pairs={{0,32},{32,64},{64,96},{1,33},{33,65},{65,97},{2,34},{34,66},{66,9... | collective-permute-start | bytes 6291464 | tf_op jit(solution)/shard_map/ppermute | solution.py:21
  127.3 48.4 %collective-permute-start.1 = (bf16[256,4096]{1,0:T(8,128)(2,1)S(1)}, bf16[256,4096]{1,0:T(8,128)(2,1)S(1)}, u32[]{:S(2)}, u32[]{:S(2)}) collective-permute-start(bf16[256,4096]{1,0:T(8,128)(2,1)S(1)} %fusion.1), channel_id=1, source_target_pairs={{0,32},{32,64},{64,96},{1,33},{33,65},{65,97},{2,34},{34,66},{66,9... | collective-permute-start | bytes 6291464 | tf_op jit(solution)/shard_map/ppermute | solution.py:21
  178.0 7.9 %copy-start.19 = (s32[4]{0:T(128)S(1)}, s32[4]{0:T(128)}, u32[]{:S(2)}) copy-start(s32[4]{0:T(128)} %param.10) | copy-start | bytes 52
  180.2 47.9 %collective-permute-start.2 = (bf16[256,4096]{1,0:T(8,128)(2,1)}, bf16[256,4096]{1,0:T(8,128)(2,1)}, u32[]{:S(2)}, u32[]{:S(2)}) collective-permute-start(bf16[256,4096]{1,0:T(8,128)(2,1)} %fusion.2), channel_id=1, source_target_pairs={{0,32},{32,64},{64,96},{1,33},{33,65},{65,97},{2,34},{34,66},{66,9... | collective-permute-start | bytes 6291464 | tf_op jit(solution)/shard_map/ppermute | solution.py:21
  186.1 43.0 %copy-start.5 = (bf16[32,1,128,2,256]{4,2,0,3,1:T(8,128)(2,1)S(1)}, bf16[32,1,128,2,256]{4,2,0,3,1:T(8,128)(2,1)}, u32[]{:S(2)}) copy-start(bf16[32,1,128,2,256]{4,2,0,3,1:T(8,128)(2,1)} %copy-done.4) | copy-start | bytes 12582916
  229.1 3.1 copy-start.11
  229.1 2.3 copy-start.1
  231.4 2.2 copy-start.10
  237.7 49.1 %collective-permute-start.3 = (bf16[256,4096]{1,0:T(8,128)(2,1)S(1)}, bf16[256,4096]{1,0:T(8,128)(2,1)S(1)}, u32[]{:S(2)}, u32[]{:S(2)}) collective-permute-start(bf16[256,4096]{1,0:T(8,128)(2,1)S(1)} %subtract_convert_fusion.2), channel_id=1, source_target_pairs={{32,0},{64,32},{96,64},{33,1},{65,33},{97,65},{34,2},{66,34},{98,6... | collective-permute-start | bytes 6291464 | tf_op jit(solution)/shard_map/ppermute | solution.py:21
  290.7 46.1 %collective-permute-start.4 = (bf16[256,4096]{1,0:T(8,128)(2,1)S(1)}, bf16[256,4096]{1,0:T(8,128)(2,1)S(1)}, u32[]{:S(2)}, u32[]{:S(2)}) collective-permute-start(bf16[256,4096]{1,0:T(8,128)(2,1)S(1)} %subtract_convert_fusion.1), channel_id=1, source_target_pairs={{32,0},{64,32},{96,64},{33,1},{65,33},{97,65},{34,2},{66,34},{98,6... | collective-permute-start | bytes 6291464 | tf_op jit(solution)/shard_map/ppermute | solution.py:21
  338.5 4.8 copy-start.20
  341.8 45.6 %collective-permute-start.5 = (bf16[256,4096]{1,0:T(8,128)(2,1)}, bf16[256,4096]{1,0:T(8,128)(2,1)}, u32[]{:S(2)}, u32[]{:S(2)}) collective-permute-start(bf16[256,4096]{1,0:T(8,128)(2,1)} %subtract_convert_fusion), channel_id=1, source_target_pairs={{32,0},{64,32},{96,64},{33,1},{65,33},{97,65},{34,2},{66,34},{98,6... | collective-permute-start | bytes 6291464 | tf_op jit(solution)/shard_map/ppermute | solution.py:21
  343.7 43.7 %copy-start.2 = (bf16[256,4096]{1,0:T(8,128)(2,1)S(1)}, bf16[256,4096]{1,0:T(8,128)(2,1)}, u32[]{:S(2)}) copy-start(bf16[256,4096]{1,0:T(8,128)(2,1)} %param.9) | copy-start | bytes 6291460
  343.7 43.7 %copy-start.6 = (bf16[32,1,128,2,256]{4,2,0,3,1:T(8,128)(2,1)S(1)}, bf16[32,1,128,2,256]{4,2,0,3,1:T(8,128)(2,1)}, u32[]{:S(2)}) copy-start(bf16[32,1,128,2,256]{4,2,0,3,1:T(8,128)(2,1)} %copy-done.4) | copy-start | bytes 12582916
  348.5 44.7 %copy-start.3 = (bf16[256,4096]{1,0:T(8,128)(2,1)}, bf16[256,4096]{1,0:T(8,128)(2,1)S(1)}, u32[]{:S(2)}) copy-start(bf16[256,4096]{1,0:T(8,128)(2,1)S(1)} %select_select_fusion.1) | copy-start | bytes 6291460
  348.5 41.6 %copy-start.13 = (bf16[256,4096]{1,0:T(8,128)(2,1)S(1)}, bf16[256,4096]{1,0:T(8,128)(2,1)}, u32[]{:S(2)}) copy-start(bf16[256,4096]{1,0:T(8,128)(2,1)} %copy-done.12) | copy-start | bytes 6291460
  348.5 41.6 %copy-start.15 = (bf16[256,4096]{1,0:T(8,128)(2,1)S(1)}, bf16[256,4096]{1,0:T(8,128)(2,1)}, u32[]{:S(2)}) copy-start(bf16[256,4096]{1,0:T(8,128)(2,1)} %copy-done.14) | copy-start | bytes 6291460
  409.1 84.0 %copy-start.16 = (f32[1,128,2,256]{3,2,1,0:T(2,128)S(1)}, f32[1,128,2,256]{3,2,1,0:T(2,128)}, u32[]{:S(2)}) copy-start(f32[1,128,2,256]{3,2,1,0:T(2,128)} %param.14) | copy-start | bytes 786436
  409.1 84.0 %copy-start.17 = (f32[1,128,2,256]{3,2,1,0:T(2,128)S(1)}, f32[1,128,2,256]{3,2,1,0:T(2,128)}, u32[]{:S(2)}) copy-start(f32[1,128,2,256]{3,2,1,0:T(2,128)} %param.15) | copy-start | bytes 786436
  (5 other events, 7.6 us)
Sparse Core Ops, SparseCore 0:
  409.2 83.7 reduce-scatter.1
